TPU v7x, 128 devices: a whole 4x4x4 slice. The times are simulated.
128 devices in a mesh: dp: 4 (over z), ctx: 32 (over y, x, core).
Axes of the slice: x: 4, y: 4, z: 4, core: 2. Of those that a mesh axis runs over, the one named last changes fastest.
Arguments:
- source_picture_sequence: bfloat16 [4, 128, 8, 8, 16, 128], P('dp', 'ctx'), may hold values from -6 to 6
- slot_assignment: int32 [128], replicated, may hold values from 0 to 127, as said below
- segment_piece_counts: int32 [16], replicated, may hold values from 1 to 16, 128 in all
- logit_scaling: float32 [4], replicated, may hold values from 1 to 16
- filter_tap_coefficients: bfloat16 [3456, 256], replicated, may hold values from -0.109375 to 0.109375
- triple_linear_matrix: bfloat16 [256, 768], replicated, may hold values from -0.375 to 0.375
- final_linear_matrix: bfloat16 [256, 256], replicated, may hold values from -0.375 to 0.375
- upstream_gradient: bfloat16 [4, 128, 4, 128, 256], P('dp', 'ctx'), may hold values from -6 to 6
Outputs:
- latents: bfloat16 [4, 128, 4, 128, 256], P('dp', 'ctx')
- conv_grad: float32 [3456, 256], P('ctx')
Inputs may be any that keep to these rules, and one draw needn't show every extreme that they name: `slot_assignment`: A permutation of the span numbers; entry i names the span at slot i, held by device i // 4. Each quarter of the span numbers, in order, fills one of the 4 positions on every device. The spans that follow one device's spans lie on at most two devices, at most two on any one device, and so do the spans that precede them; in every draw some device has two spans followed by spans on one other device.
All inputs are finite; a program needn't handle non-finite values.
Results may differ from a plain program's by a relative error of at most 0.0058.
Values may be sent and summed in bfloat16 or wider, within the bound.
A program may use at most 128 MiB of HBM per device.

v0:
```python
import jax
import jax.numpy as jnp
from jax import lax
from jax.sharding import PartitionSpec as P

masked_score = -1e30


def clip_marks(segment_piece_counts, span_ids):
    clip_ends = jnp.cumsum(segment_piece_counts, dtype=jnp.int32)
    clip_starts = clip_ends - segment_piece_counts
    clip_index = jnp.sum(
        (span_ids[:, None] >= clip_ends[None, :]).astype(jnp.int32), axis=1, dtype=jnp.int32
    )
    opening = jnp.any(span_ids[:, None] == clip_starts[None, :], axis=1)
    return (clip_index, opening)


def locate(span_ids, slot_assignment):
    slot_ids = jnp.arange(slot_assignment.shape[0], dtype=jnp.int32)
    matches = slot_assignment[None, :] == span_ids[:, None]
    return jnp.sum(jnp.where(matches, slot_ids[None, :], 0), axis=1, dtype=jnp.int32)


def conv_patches(frames):
    span_total, unused_len, rows_h, cols_w, channel_in = frames.shape
    padded = jnp.pad(frames, ((0, 0), (0, 0), (1, 1), (1, 1), (0, 0)))
    tap_list = []
    for step_t in range(3):
        for step_h in range(3):
            for step_w in range(3):
                tap_list.append(
                    padded[
                        :,
                        step_t : step_t + 7 : 2,
                        step_h : step_h + rows_h,
                        step_w : step_w + cols_w,
                        :,
                    ]
                )
    return jnp.concatenate(tap_list, axis=-1).reshape(-1, 27 * channel_in)


def timewise_softmax_mixing(
    grid_tile_entries, logit_scaling, triple_linear_matrix, final_linear_matrix, allowance_pattern
):
    channel_width = grid_tile_entries.shape[-1]
    channel_group_index = logit_scaling.shape[0]
    head_size = channel_width // channel_group_index
    values32 = grid_tile_entries.astype(jnp.float32)
    normed = (
        values32 * lax.rsqrt(jnp.mean(values32 * values32, axis=-1, keepdims=True) + 1e-06)
    ).astype(jnp.bfloat16)
    projected = jnp.einsum(
        "gac,cd->gad", normed, triple_linear_matrix, preferred_element_type=jnp.float32
    )
    head_shape = grid_tile_entries.shape[:2] + (channel_group_index, head_size)
    queries = projected[..., :channel_width].reshape(head_shape)
    keys_all = projected[..., channel_width : 2 * channel_width].reshape(head_shape)
    head_values = projected[..., 2 * channel_width :].reshape(head_shape).astype(jnp.bfloat16)
    queries = queries * lax.rsqrt(jnp.sum(queries * queries, axis=-1, keepdims=True) + 1e-06)
    keys_all = keys_all * lax.rsqrt(jnp.sum(keys_all * keys_all, axis=-1, keepdims=True) + 1e-06)
    affinity_logits = jnp.einsum(
        "gahd,gbhd->ghab", queries, keys_all, precision=lax.Precision.HIGHEST
    )
    affinity_logits = affinity_logits * logit_scaling[None, :, None, None]
    affinity_logits = jnp.where(allowance_pattern[None, None], affinity_logits, masked_score)
    highest = jnp.max(affinity_logits, axis=-1, keepdims=True)
    weights = jnp.exp(affinity_logits - highest)
    probabilities = (weights / jnp.sum(weights, axis=-1, keepdims=True)).astype(jnp.bfloat16)
    mixed_heads = jnp.einsum(
        "ghab,gbhd->gahd", probabilities, head_values, preferred_element_type=jnp.float32
    )
    mixed_heads = mixed_heads.astype(jnp.bfloat16).reshape(grid_tile_entries.shape)
    branch = jnp.einsum(
        "gac,cd->gad", mixed_heads, final_linear_matrix, preferred_element_type=jnp.float32
    )
    return (values32 + branch).astype(jnp.bfloat16)


def per_device(
    source_picture_sequence,
    slot_assignment,
    segment_piece_counts,
    logit_scaling,
    filter_tap_coefficients,
    triple_linear_matrix,
    final_linear_matrix,
    upstream_gradient,
):
    my_index = lax.axis_index("ctx")
    local_frames = source_picture_sequence[0]
    slot_count = local_frames.shape[0]
    my_spans = lax.dynamic_slice_in_dim(slot_assignment, my_index * slot_count, slot_count)
    unused_clip, opening = clip_marks(segment_piece_counts, my_spans)
    pred_slot = locate(jnp.maximum(my_spans - 1, 0), slot_assignment)
    tails = local_frames[:, 6:]
    shard_rows = lax.all_gather(tails, "ctx", axis=0, tiled=True)
    inside = (pred_slot >= 0) & (pred_slot < shard_rows.shape[0])
    chosen = shard_rows[jnp.clip(pred_slot, 0, shard_rows.shape[0] - 1)]
    previous = jnp.where(inside[:, None, None, None, None], chosen, jnp.zeros_like(tails))
    previous = jnp.where(opening[:, None, None, None, None], jnp.zeros_like(previous), previous)
    patches = conv_patches(jnp.concatenate([previous, local_frames], axis=1))
    channels = filter_tap_coefficients.shape[1]
    cell_count = local_frames.shape[2] * local_frames.shape[3]
    conv_out = jnp.dot(patches, filter_tap_coefficients, preferred_element_type=jnp.float32).astype(
        jnp.bfloat16
    )
    conv_out = conv_out.reshape(slot_count, 4, cell_count, channels)
    grad_rows = upstream_gradient[0].reshape(-1, channels)
    grad_share = lax.psum_scatter(
        jnp.dot(patches.T, grad_rows, preferred_element_type=jnp.float32),
        "ctx",
        scatter_dimension=0,
        tiled=True,
    )
    conv_grad = lax.psum(grad_share, "dp")
    gathered = lax.all_to_all(conv_out, "ctx", split_axis=2, concat_axis=0, tiled=True)
    frame_total = gathered.shape[0] * 4
    cells_dev = gathered.shape[2]
    location_entry_count = jnp.transpose(
        gathered.reshape(frame_total, cells_dev, channels), (1, 0, 2)
    )
    clip_all, unused_open = clip_marks(segment_piece_counts, slot_assignment)
    frame_clip = jnp.repeat(clip_all, 4)
    frame_time = (slot_assignment[:, None] * 4 + jnp.arange(4, dtype=jnp.int32)[None, :]).reshape(
        -1
    )
    allowance_pattern = (frame_clip[:, None] == frame_clip[None, :]) & (
        frame_time[None, :] <= frame_time[:, None]
    )
    cell_group = 1
    block_list = location_entry_count.reshape(
        cells_dev // cell_group, cell_group, frame_total, channels
    )
    blended_result = lax.map(
        lambda grid_tile_entries: timewise_softmax_mixing(
            grid_tile_entries,
            logit_scaling,
            triple_linear_matrix,
            final_linear_matrix,
            allowance_pattern,
        ),
        block_list,
    )
    blended_result = jnp.transpose(
        blended_result.reshape(cells_dev, frame_total, channels), (1, 0, 2)
    ).reshape(gathered.shape)
    latents = lax.all_to_all(blended_result, "ctx", split_axis=0, concat_axis=2, tiled=True)
    return (latents[None], conv_grad)


def solution(mesh):
    placed = (
        P("dp", "ctx", None, None, None, None),
        P(),
        P(),
        P(),
        P(),
        P(),
        P(),
        P("dp", "ctx", None, None, None),
    )
    return jax.shard_map(
        per_device,
        mesh=mesh,
        in_specs=placed,
        out_specs=(P("dp", "ctx", None, None, None), P("ctx", None)),
        check_vma=False,
    )
```

profile of v0, /device:TPU:0, one launch (start us, length us, event | category | flops | bytes accessed | tf_op | source)
XLA Modules:
  0.0 376.9 jit_solution(8046809622749582942)
XLA Ops:
  14.2 51.2 %all-gather.2.cloned.1.call-done = bf16[128,2,8,16,128]{4,3,2,1,0:T(8,128)(2,1)} async-done(((bf16[4,2,8,16,128]{4,3,2,1,0:T(8,128)(2,1)}), bf16[128,2,8,16,128]{4,3,2,1,0:T(8,128)(2,1)}) %all-gather.2.cloned.1.call-update) | async-done | bytes 8388624 | tf_op jit(solution)/shard_map/all_gather | solution.py:98
  65.4 4.0 %gather_fusion = bf16[4,2,8,16,128]{4,3,2,1,0:T(8,128)(2,1)S(1)} fusion(bf16[128,2,8,16,128]{4,3,2,1,0:T(8,128)(2,1)} %all-gather.2.cloned.1.call-done, s32[1024]{0:T(1024)S(1)} %pad_clamp_fusion), kind=kCustom, calls=%fused_computation | custom fusion | bytes 524304 | tf_op jit(solution)/shard_map/gather | solution.py:100
  78.5 4.1 %convolution_convert_fusion = bf16[2048,256]{1,0:T(8,128)(2,1)S(1)} fusion(bf16[2048,3456]{1,0:T(8,128)(2,1)S(1)} %bitcast.102, bf16[3456,256]{1,0:T(8,128)(2,1)S(1)} %copy-done), kind=kOutput, calls=%fused_computation.47 | convolution fusion | flops 3624402944 | bytes 16973824 | tf_op jit(solution)/shard_map/dot_general | solution.py:106
  85.3 5.6 %all-to-all-start = ((bf16[4,4,128,256]{3,1,0,2:T(4,128)(2,1)}), bf16[4,4,128,256]{3,1,0,2:T(4,128)(2,1)S(1)}, u32[]{:S(2)}, u32[]{:S(2)}) async-start(bf16[4,4,128,256]{3,1,0,2:T(4,128)(2,1)} %copy.55), calls=%async_computation | async-start | bytes 2097152 | tf_op jit(solution)/shard_map/all_to_all | solution.py:118
  91.0 10.9 %fusion.36 = f32[3456,256]{1,0:T(8,128)} fusion(bf16[2048,3456]{1,0:T(8,128)(2,1)} %bitcast.103, bf16[2048,256]{1,0:T(8,128)(2,1)} %bitcast.105), kind=kOutput, calls=%fused_computation.91 | convolution fusion | flops 3623878656 | bytes 18743296 | tf_op jit(solution)/shard_map/dot_general | solution.py:112
  101.9 6.1 %all-to-all-done = bf16[4,4,128,256]{3,1,0,2:T(4,128)(2,1)S(1)} async-done(((bf16[4,4,128,256]{3,1,0,2:T(4,128)(2,1)}), bf16[4,4,128,256]{3,1,0,2:T(4,128)(2,1)S(1)}, u32[]{:S(2)}, u32[]{:S(2)}) %all-to-all-start) | async-done | bytes 1048608 | tf_op jit(solution)/shard_map/all_to_all | solution.py:118
  109.4 2.1 reshape.266
  111.6 120.4 %while.11 = (s32[]{:T(128)}, bf16[4,1,512,256]{3,2,1,0:T(8,128)(2,1)}, bf16[4,1,512,256]{3,2,1,0:T(8,128)(2,1)}, bf16[256,768]{1,0:T(8,128)(2,1)}, f32[4]{0:T(12...) while((s32[]{:T(128)}, ...), condition=%wide.region_10.11_spmd.clone, body=%wide.region_4.10_spmd.clone.sunk | while | flops 1219232768 | bytes 31814784 | solution.py:136
  126.1 4.7 %fusion.65 = f32[4,512,512]{1,2,0:T(8,128)S(1)} fusion(f32[512,4,64]{0,2,1:T(8,128)} %bitcast.89, f32[512,4,64]{0,2,1:T(8,128)} %bitcast.90, f32[512,4]{0,1:T(4,128)S(1)} %get-tuple-element.153, f32[512,4]{0,1:T(4,128)S(1)} %get-tuple-element.154), kind=kOutput, calls=%fused_computation.24.clone.1 | convolution fusion | flops 805568512 | bytes 5259264 | tf_op jit(solution)/shard_map/while/body/eval_jaxpr/gahd,gbhd->ghab/dot_general | solution.py:63
  131.1 4.2 %fusion.66 = (f32[4,512]{1,0:T(4,128)S(1)}, f32[4,512,512]{1,2,0:T(8,128)}) fusion(f32[4,512,512]{1,2,0:T(8,128)S(1)} %fusion.65, f32[4]{0:T(128)S(1)} %get-tuple-element.181, pred[512,512]{0,1:T(8,128)(4,1)S(1)} %compare_and_fusion.3), kind=kOutput, calls=%fused_computation.90.clone.1 | output fusion | flops 6291967 | bytes 8658960 | tf_op jit(solution)/shard_map/while/body/eval_jaxpr/sub | solution.py:69
  137.0 2.7 fusion.67
  156.1 4.7 %fusion.65 = f32[4,512,512]{1,2,0:T(8,128)S(1)} fusion(f32[512,4,64]{0,2,1:T(8,128)} %bitcast.89, f32[512,4,64]{0,2,1:T(8,128)} %bitcast.90, f32[512,4]{0,1:T(4,128)S(1)} %get-tuple-element.153, f32[512,4]{0,1:T(4,128)S(1)} %get-tuple-element.154), kind=kOutput, calls=%fused_computation.24.clone.1 | convolution fusion | flops 805568512 | bytes 5259264 | tf_op jit(solution)/shard_map/while/body/eval_jaxpr/gahd,gbhd->ghab/dot_general | solution.py:63
  161.2 4.2 %fusion.66 = (f32[4,512]{1,0:T(4,128)S(1)}, f32[4,512,512]{1,2,0:T(8,128)}) fusion(f32[4,512,512]{1,2,0:T(8,128)S(1)} %fusion.65, f32[4]{0:T(128)S(1)} %get-tuple-element.181, pred[512,512]{0,1:T(8,128)(4,1)S(1)} %compare_and_fusion.3), kind=kOutput, calls=%fused_computation.90.clone.1 | output fusion | flops 6291967 | bytes 8658960 | tf_op jit(solution)/shard_map/while/body/eval_jaxpr/sub | solution.py:69
  167.1 2.7 fusion.67
  186.2 4.7 %fusion.65 = f32[4,512,512]{1,2,0:T(8,128)S(1)} fusion(f32[512,4,64]{0,2,1:T(8,128)} %bitcast.89, f32[512,4,64]{0,2,1:T(8,128)} %bitcast.90, f32[512,4]{0,1:T(4,128)S(1)} %get-tuple-element.153, f32[512,4]{0,1:T(4,128)S(1)} %get-tuple-element.154), kind=kOutput, calls=%fused_computation.24.clone.1 | convolution fusion | flops 805568512 | bytes 5259264 | tf_op jit(solution)/shard_map/while/body/eval_jaxpr/gahd,gbhd->ghab/dot_general | solution.py:63
  191.2 4.2 %fusion.66 = (f32[4,512]{1,0:T(4,128)S(1)}, f32[4,512,512]{1,2,0:T(8,128)}) fusion(f32[4,512,512]{1,2,0:T(8,128)S(1)} %fusion.65, f32[4]{0:T(128)S(1)} %get-tuple-element.181, pred[512,512]{0,1:T(8,128)(4,1)S(1)} %compare_and_fusion.3), kind=kOutput, calls=%fused_computation.90.clone.1 | output fusion | flops 6291967 | bytes 8658960 | tf_op jit(solution)/shard_map/while/body/eval_jaxpr/sub | solution.py:69
  197.2 2.7 fusion.67
  216.3 4.7 %fusion.65 = f32[4,512,512]{1,2,0:T(8,128)S(1)} fusion(f32[512,4,64]{0,2,1:T(8,128)} %bitcast.89, f32[512,4,64]{0,2,1:T(8,128)} %bitcast.90, f32[512,4]{0,1:T(4,128)S(1)} %get-tuple-element.153, f32[512,4]{0,1:T(4,128)S(1)} %get-tuple-element.154), kind=kOutput, calls=%fused_computation.24.clone.1 | convolution fusion | flops 805568512 | bytes 5259264 | tf_op jit(solution)/shard_map/while/body/eval_jaxpr/gahd,gbhd->ghab/dot_general | solution.py:63
  221.3 4.2 %fusion.66 = (f32[4,512]{1,0:T(4,128)S(1)}, f32[4,512,512]{1,2,0:T(8,128)}) fusion(f32[4,512,512]{1,2,0:T(8,128)S(1)} %fusion.65, f32[4]{0:T(128)S(1)} %get-tuple-element.181, pred[512,512]{0,1:T(8,128)(4,1)S(1)} %compare_and_fusion.3), kind=kOutput, calls=%fused_computation.90.clone.1 | output fusion | flops 6291967 | bytes 8658960 | tf_op jit(solution)/shard_map/while/body/eval_jaxpr/sub | solution.py:69
  227.3 2.7 fusion.67
  231.9 3.0 copy.61
  235.0 3.9 %all-to-all-start.1 = ((bf16[128,4,4,256]{3,2,1,0:T(4,128)(2,1)}), bf16[128,4,4,256]{3,2,1,0:T(4,128)(2,1)S(1)}, u32[]{:S(2)}, u32[]{:S(2)}) async-start(bf16[128,4,4,256]{3,2,1,0:T(4,128)(2,1)} %bitcast.95), calls=%async_computation.1 | async-start | bytes 2097152 | tf_op jit(solution)/shard_map/all_to_all | solution.py:149
  238.9 84.1 %fusion.2 = f32[112,256]{1,0:T(8,128)S(1)} fusion(f32[3456,256]{1,0:T(8,128)} %fusion.36), kind=kCustom, calls=%all-reduce-scatter | all-reduce-scatter fusion | flops 917505 | bytes 3654144
  329.8 38.7 %all-reduce.5.cloned.1.call-done = f32[108,256]{1,0:T(8,128)} async-done(((f32[108,256]{1,0:T(8,128)}), f32[108,256]{1,0:T(8,128)}) %all-reduce.5.cloned.1.call-update) | async-done | bytes 110608 | tf_op jit(solution)/shard_map/psum | solution.py:117
  (135 shorter events, 101.5 us)
Async XLA Ops:
  7.2 71.3 %copy-start = (bf16[3456,256]{1,0:T(8,128)(2,1)S(1)}, bf16[3456,256]{1,0:T(8,128)(2,1)}, u32[]{:S(2)}) copy-start(bf16[3456,256]{1,0:T(8,128)(2,1)} %param.14) | copy-start | bytes 5308420
  7.2 58.2 %all-gather.2.cloned.1.call-start = ((), (), s32[]{:S(2)}) async-start(), calls=%async_computation.2 | async-start | bytes 8650752 | tf_op jit(solution)/shard_map/all_gather | solution.py:98
  78.5 5.1 %copy-start.1 = (bf16[4,4,8,16,3456]{4,3,2,1,0:T(8,128)(2,1)}, bf16[4,4,8,16,3456]{4,3,2,1,0:T(8,128)(2,1)S(1)}, u32[]{:S(2)}) copy-start(bf16[4,4,8,16,3456]{4,3,2,1,0:T(8,128)(2,1)S(1)} %slice_dynamic-update-slice_fusion) | copy-start | bytes 42467332
  85.3 22.7 %all-to-all-start = ((bf16[4,4,128,256]{3,1,0,2:T(4,128)(2,1)}), bf16[4,4,128,256]{3,1,0,2:T(4,128)(2,1)S(1)}, u32[]{:S(2)}, u32[]{:S(2)}) async-start(bf16[4,4,128,256]{3,1,0,2:T(4,128)(2,1)} %copy.55), calls=%async_computation | async-start | bytes 2097152 | tf_op jit(solution)/shard_map/all_to_all | solution.py:118
  91.0 20.6 %copy-start.3 = (bf16[256,256]{1,0:T(8,128)(2,1)S(1)}, bf16[256,256]{1,0:T(8,128)(2,1)}, u32[]{:S(2)}) copy-start(bf16[256,256]{1,0:T(8,128)(2,1)} %param.16) | copy-start | bytes 393220
  91.0 20.6 %copy-start.4 = (f32[4]{0:T(128)S(1)}, f32[4]{0:T(128)}, u32[]{:S(2)}) copy-start(f32[4]{0:T(128)} %param.13) | copy-start | bytes 52
  111.5 214.1 %copy-start.2 = (u32[128]{0:T(128)S(1)}, u32[128]{0:T(128)}, u32[]{:S(2)}) copy-start(u32[128]{0:T(128)} %constant.55) | copy-start | bytes 1540
  235.0 93.2 %all-to-all-start.1 = ((bf16[128,4,4,256]{3,2,1,0:T(4,128)(2,1)}), bf16[128,4,4,256]{3,2,1,0:T(4,128)(2,1)S(1)}, u32[]{:S(2)}, u32[]{:S(2)}) async-start(bf16[128,4,4,256]{3,2,1,0:T(4,128)(2,1)} %bitcast.95), calls=%async_computation.1 | async-start | bytes 2097152 | tf_op jit(solution)/shard_map/all_to_all | solution.py:149
  238.9 129.6 %all-reduce.5.cloned.1.call-start = ((), (), s32[]{:S(2)}) async-start(), calls=%async_computation.3 | async-start | bytes 229376 | tf_op jit(solution)/shard_map/psum | solution.py:117
  323.0 4.0 %collective-permute-start = (f32[112,256]{1,0:T(8,128)S(1)}, f32[112,256]{1,0:T(8,128)S(1)}, u32[]{:S(2)}, u32[]{:S(2)}) collective-permute-start(f32[112,256]{1,0:T(8,128)S(1)} %fusion.2), channel_id=1, source_target_pairs={{0,1},{1,2},{2,3},{3,4},{4,5},{5,6},{6,7},{7,8},{8,9},{9,10},{10,1... | collective-permute-start | bytes 344072
  324.3 2.7 collective-permute-start.1
Sparse Core Ops, SparseCore 0:
  10.3 55.1 all-gather.1
  328.3 40.1 all-reduce.4
where the time goes:
time: 379 us; the launch traced here: 377 us
  waiting for transfers between devices  96.2 us (25%)
  blocking collectives  84.1 us (22%)
  local copies, waits for them, and re-layouts  67.8 us (18%)
  matrix products  58.3 us (15%)
  other arithmetic  42.9 us (11%)
  between operations  15.1 us (4%)
  starting transfers between devices  12.2 us (3%)
    unnamed x1, blocking collectives  84.1 us
    all_gather x1, waiting for transfers between devices, per_device(): shard_rows = lax.all_gather(tails, 'ctx', axis=0, tiled=True)  51.2 us
    psum x1, waiting for transfers between devices, per_device(): conv_grad = lax.psum(grad_share, 'dp')  38.7 us
    dot_general x4, matrix products, timewise_softmax_mixing(): jnp.einsum('gahd,gbhd->ghab', queries, keys_all, precision=lax.Precision....  18.9 us
    sub x4, other arithmetic, timewise_softmax_mixing(): weights = jnp.exp(affinity_logits - highest)  16.6 us
    unnamed x42, local copies, waits for them, and re-layouts  11.7 us
    dot_general x1, matrix products, per_device(): jnp.dot(patches.T, grad_rows, preferred_element_type=jnp.float32)  10.9 us
    dot_general x4, matrix products, timewise_softmax_mixing(): jnp.einsum('ghab,gbhd->gahd', probabilities, head_values, preferred_eleme...  10.7 us
  transfers between devices with their start and end apart: 6, of which 4 were waited for; matrix products, arithmetic and copies ran while one was open for 27% of the time, Pallas kernels for 0%

commit v1 on v0

--- a/solution.py
+++ b/solution.py
@@ -95,7 +95,9 @@
     unused_clip, opening = clip_marks(segment_piece_counts, my_spans)
     pred_slot = locate(jnp.maximum(my_spans - 1, 0), slot_assignment)
     tails = local_frames[:, 6:]
-    shard_rows = lax.all_gather(tails, "ctx", axis=0, tiled=True)
+    shard_rows = jnp.concatenate(
+        lax.all_to_all(jnp.stack([tails] * lax.axis_size("ctx")), "ctx", 0, 0), axis=0
+    )
     inside = (pred_slot >= 0) & (pred_slot < shard_rows.shape[0])
     chosen = shard_rows[jnp.clip(pred_slot, 0, shard_rows.shape[0] - 1)]
     previous = jnp.where(inside[:, None, None, None, None], chosen, jnp.zeros_like(tails))

time: 379 us -> 395 us (1.042)
  waiting for transfers between devices: 96.2 us -> 152 us
  local copies, waits for them, and re-layouts: 67.8 us -> 41.9 us
  other arithmetic: 42.9 us -> 29.3 us
  matrix products: 58.3 us -> 51.6 us
  starting transfers between devices: 12.2 us -> 18.4 us
    all_to_all x0 -> x1, waiting for transfers between devices: none -> 105 us  [per_device(): lax.all_to_all(jnp.stack([tails] * lax.axis_size('ctx')), 'ctx', 0, 0)]
    all_gather x1 -> x0, waiting for transfers between devices: 51.2 us -> none  [per_device(): shard_rows = lax.all_gather(tails, 'ctx', axis=0, tiled=True)]
    all_to_all x0 -> x1, starting transfers between devices: none -> 7.69 us  [per_device(): lax.all_to_all(jnp.stack([tails] * lax.axis_size('ctx')), 'ctx', 0, 0)]
    slice x4, local copies, waits for them, and re-layouts: 8.24 us -> 0.79 us  [timewise_softmax_mixing(): projected[..., channel_width:2 * channel_width].reshape(head_shape)]
    slice x4, local copies, waits for them, and re-layouts: 8.21 us -> 0.79 us  [timewise_softmax_mixing(): queries = projected[..., :channel_width].reshape(head_shape)]
    slice x8, local copies, waits for them, and re-layouts: 7.29 us -> 0.67 us  [timewise_softmax_mixing(): projected[..., 2 * channel_width:].reshape(head_shape).astype(jnp.bfloat16)]
    dot_general x4, matrix products: 18.9 us -> 14.1 us  [timewise_softmax_mixing(): jnp.einsum('gahd,gbhd->ghab', queries, keys_all, precision=lax.Precision....]
    another operation x1 -> x2, local copies, waits for them, and re-layouts: 0.73 us -> 5.42 us  [the longest x1 5.34 us: per_device(): jnp.stack([tails] * lax.axis_size('ctx'))]
  transfers between devices with their start and end apart: 6 -> 6, of which waited for: 4 -> 4; matrix products, arithmetic and copies ran while one was open for 27% -> 25% of each run, Pallas kernels for 0% -> 0%
where the time goes in v1:
time: 395 us; the launch traced here: 393 us
  waiting for transfers between devices  152 us (38%)
  blocking collectives  84.1 us (21%)
  matrix products  51.6 us (13%)
  local copies, waits for them, and re-layouts  41.9 us (11%)
  other arithmetic  29.3 us (7%)
  starting transfers between devices  18.4 us (5%)
  between operations  15.1 us (4%)
    all_to_all x1, waiting for transfers between devices, per_device(): lax.all_to_all(jnp.stack([tails] * lax.axis_size('ctx')), 'ctx', 0, 0)  105 us
    unnamed x1, blocking collectives  84.1 us
    psum x1, waiting for transfers between devices, per_device(): conv_grad = lax.psum(grad_share, 'dp')  39.6 us
    sub x4, other arithmetic, timewise_softmax_mixing(): weights = jnp.exp(affinity_logits - highest)  16.6 us
    dot_general x4, matrix products, timewise_softmax_mixing(): jnp.einsum('gahd,gbhd->ghab', queries, keys_all, precision=lax.Precision....  14.1 us
    unnamed x52, local copies, waits for them, and re-layouts  11.7 us
    dot_general x4, matrix products, timewise_softmax_mixing(): jnp.einsum('ghab,gbhd->gahd', probabilities, head_values, preferred_eleme...  10.7 us
    dot_general x1, matrix products, per_device(): jnp.dot(patches.T, grad_rows, preferred_element_type=jnp.float32)  8.91 us
  transfers between devices with their start and end apart: 6, of which 4 were waited for; matrix products, arithmetic and copies ran while one was open for 25% of the time, Pallas kernels for 0%

profile of v1, /device:TPU:0, one launch (start us, length us, event | category | flops | bytes accessed | tf_op | source)
XLA Modules:
  0.0 393.2 jit_solution(14491223263736302168)
XLA Ops:
  8.3 5.3 %stack.2 = bf16[32,4,2,8,16,128]{5,4,3,2,1,0:T(8,128)(2,1)} broadcast(bf16[4,2,8,16,128]{4,3,2,1,0:T(8,128)(2,1)S(1)} %slice.130), dimensions={1,2,3,4,5} | broadcast | bytes 8650752 | tf_op jit(solution)/shard_map/stack | solution.py:99
  13.6 7.7 %all-to-all-start = ((bf16[32,4,2,8,16,128]{5,4,3,2,1,0:T(8,128)(2,1)}), bf16[32,4,2,8,16,128]{5,4,3,2,1,0:T(8,128)(2,1)}, u32[]{:S(2)}, u32[]{:S(2)}) async-start(bf16[32,4,2,8,16,128]{5,4,3,2,1,0:T(8,128)(2,1)} %stack.2), calls=%async_computation | async-start | bytes 16777216 | tf_op jit(solution)/shard_map/all_to_all | solution.py:99
  22.6 104.6 %all-to-all-done = bf16[32,4,2,8,16,128]{5,4,3,2,1,0:T(8,128)(2,1)} async-done(((bf16[32,4,2,8,16,128]{5,4,3,2,1,0:T(8,128)(2,1)}), bf16[32,4,2,8,16,128]{5,4,3,2,1,0:T(8,128)(2,1)}, u32[]{:S(2)}, u32[]{:S(2)}) %all-to-all-start) | async-done | bytes 8388640 | tf_op jit(solution)/shard_map/all_to_all | solution.py:99
  127.2 4.0 %gather_fusion = bf16[4,2,8,16,128]{4,3,2,1,0:T(8,128)(2,1)S(1)} fusion(bf16[128,2,8,16,128]{4,3,2,1,0:T(8,128)(2,1)} %bitcast.2, s32[1024]{0:T(1024)S(1)} %pad_clamp_fusion), kind=kCustom, calls=%fused_computation | custom fusion | bytes 524304 | tf_op jit(solution)/shard_map/gather | solution.py:102
  139.4 4.1 %convolution_convert_fusion = bf16[2048,256]{1,0:T(8,128)(2,1)S(1)} fusion(bf16[2048,3456]{1,0:T(8,128)(2,1)S(1)} %bitcast.103, bf16[3456,256]{1,0:T(8,128)(2,1)S(1)} %copy-done), kind=kOutput, calls=%fused_computation.47 | convolution fusion | flops 3624402944 | bytes 16973824 | tf_op jit(solution)/shard_map/dot_general | solution.py:108
  146.2 4.1 %all-to-all-start.1 = ((bf16[4,4,128,256]{3,1,0,2:T(4,128)(2,1)}), bf16[4,4,128,256]{3,1,0,2:T(4,128)(2,1)S(1)}, u32[]{:S(2)}, u32[]{:S(2)}) async-start(bf16[4,4,128,256]{3,1,0,2:T(4,128)(2,1)} %copy.55), calls=%async_computation.1 | async-start | bytes 2097152 | tf_op jit(solution)/shard_map/all_to_all | solution.py:120
  150.4 8.9 %fusion.36 = f32[3456,256]{1,0:T(8,128)} fusion(bf16[2048,3456]{1,0:T(8,128)(2,1)} %bitcast.104, bf16[2048,256]{1,0:T(8,128)(2,1)S(1)} %bitcast.106), kind=kOutput, calls=%fused_computation.91 | convolution fusion | flops 3623878656 | bytes 18743296 | tf_op jit(solution)/shard_map/dot_general | solution.py:114
  159.3 8.0 %all-to-all-done.1 = bf16[4,4,128,256]{3,1,0,2:T(4,128)(2,1)S(1)} async-done(((bf16[4,4,128,256]{3,1,0,2:T(4,128)(2,1)}), bf16[4,4,128,256]{3,1,0,2:T(4,128)(2,1)S(1)}, u32[]{:S(2)}, u32[]{:S(2)}) %all-to-all-start.1) | async-done | bytes 1048608 | tf_op jit(solution)/shard_map/all_to_all | solution.py:120
  168.9 78.3 %while.11 = (s32[]{:T(128)}, bf16[4,1,512,256]{3,2,1,0:T(8,128)(2,1)}, bf16[4,1,512,256]{3,2,1,0:T(8,128)(2,1)}, bf16[256,768]{1,0:T(8,128)(2,1)}, f32[4]{0:T(12...) while((s32[]{:T(128)}, ...), condition=%wide.region_10.11_spmd.clone, body=%wide.region_4.10_spmd.clone.sunk | while | flops 1219232768 | bytes 31814784 | solution.py:138
  175.7 3.5 fusion.65
  179.6 4.2 %fusion.66 = (f32[4,512]{1,0:T(4,128)S(1)}, f32[4,512,512]{1,2,0:T(8,128)}) fusion(f32[4,512,512]{1,2,0:T(8,128)S(1)} %fusion.65, f32[4]{0:T(128)S(1)} %get-tuple-element.181, pred[512,512]{0,1:T(8,128)(4,1)S(1)} %compare_and_fusion.3), kind=kOutput, calls=%fused_computation.90.clone.1 | output fusion | flops 6291967 | bytes 8658960 | tf_op jit(solution)/shard_map/while/body/eval_jaxpr/sub | solution.py:69
  183.9 2.7 fusion.67
  195.3 3.5 fusion.65
  199.1 4.2 %fusion.66 = (f32[4,512]{1,0:T(4,128)S(1)}, f32[4,512,512]{1,2,0:T(8,128)}) fusion(f32[4,512,512]{1,2,0:T(8,128)S(1)} %fusion.65, f32[4]{0:T(128)S(1)} %get-tuple-element.181, pred[512,512]{0,1:T(8,128)(4,1)S(1)} %compare_and_fusion.3), kind=kOutput, calls=%fused_computation.90.clone.1 | output fusion | flops 6291967 | bytes 8658960 | tf_op jit(solution)/shard_map/while/body/eval_jaxpr/sub | solution.py:69
  214.9 3.5 fusion.65
  218.7 4.2 %fusion.66 = (f32[4,512]{1,0:T(4,128)S(1)}, f32[4,512,512]{1,2,0:T(8,128)}) fusion(f32[4,512,512]{1,2,0:T(8,128)S(1)} %fusion.65, f32[4]{0:T(128)S(1)} %get-tuple-element.181, pred[512,512]{0,1:T(8,128)(4,1)S(1)} %compare_and_fusion.3), kind=kOutput, calls=%fused_computation.90.clone.1 | output fusion | flops 6291967 | bytes 8658960 | tf_op jit(solution)/shard_map/while/body/eval_jaxpr/sub | solution.py:69
  223.0 2.7 fusion.67
  234.5 3.5 fusion.65
  238.3 4.2 %fusion.66 = (f32[4,512]{1,0:T(4,128)S(1)}, f32[4,512,512]{1,2,0:T(8,128)}) fusion(f32[4,512,512]{1,2,0:T(8,128)S(1)} %fusion.65, f32[4]{0:T(128)S(1)} %get-tuple-element.181, pred[512,512]{0,1:T(8,128)(4,1)S(1)} %compare_and_fusion.3), kind=kOutput, calls=%fused_computation.90.clone.1 | output fusion | flops 6291967 | bytes 8658960 | tf_op jit(solution)/shard_map/while/body/eval_jaxpr/sub | solution.py:69
  242.6 2.7 fusion.67
  247.2 3.2 copy.61
  250.4 3.9 all-to-all-start.2
  254.4 84.1 %fusion.2 = f32[112,256]{1,0:T(8,128)S(1)} fusion(f32[3456,256]{1,0:T(8,128)} %fusion.36), kind=kCustom, calls=%all-reduce-scatter | all-reduce-scatter fusion | flops 917505 | bytes 3654144
  345.2 39.6 %all-reduce.5.cloned.1.call-done = f32[108,256]{1,0:T(8,128)} async-done(((f32[108,256]{1,0:T(8,128)}), f32[108,256]{1,0:T(8,128)}) %all-reduce.5.cloned.1.call-update) | async-done | bytes 110608 | tf_op jit(solution)/shard_map/psum | solution.py:119
  (145 shorter events, 61.4 us)
Async XLA Ops:
  7.2 132.2 %copy-start = (bf16[3456,256]{1,0:T(8,128)(2,1)S(1)}, bf16[3456,256]{1,0:T(8,128)(2,1)}, u32[]{:S(2)}) copy-start(bf16[3456,256]{1,0:T(8,128)(2,1)} %param.14) | copy-start | bytes 5308420
  13.6 7.7 %copy-start.4 = (s32[16]{0:T(128)S(1)}, s32[16]{0:T(128)}, u32[]{:S(2)}) copy-start(s32[16]{0:T(128)} %param.12) | copy-start | bytes 196
  13.6 8.0 %copy-start.6 = (s32[128]{0:T(128)S(1)}, s32[128]{0:T(128)}, u32[]{:S(2)}) copy-start(s32[128]{0:T(128)} %param.11) | copy-start | bytes 1540
  13.6 117.7 %copy-start.2 = (bf16[1,4,8,8,16,128]{5,4,3,2,1,0:T(8,128)(2,1)S(1)}, bf16[1,4,8,8,16,128]{5,4,3,2,1,0:T(8,128)(2,1)}, u32[]{:S(2)}) copy-start(bf16[1,4,8,8,16,128]{5,4,3,2,1,0:T(8,128)(2,1)} %param.10) | copy-start | bytes 3145732
  13.6 113.6 %all-to-all-start = ((bf16[32,4,2,8,16,128]{5,4,3,2,1,0:T(8,128)(2,1)}), bf16[32,4,2,8,16,128]{5,4,3,2,1,0:T(8,128)(2,1)}, u32[]{:S(2)}, u32[]{:S(2)}) async-start(bf16[32,4,2,8,16,128]{5,4,3,2,1,0:T(8,128)(2,1)} %stack.2), calls=%async_computation | async-start | bytes 16777216 | tf_op jit(solution)/shard_map/all_to_all | solution.py:99
  139.4 5.1 %copy-start.3 = (bf16[4,4,8,16,3456]{4,3,2,1,0:T(8,128)(2,1)}, bf16[4,4,8,16,3456]{4,3,2,1,0:T(8,128)(2,1)S(1)}, u32[]{:S(2)}) copy-start(bf16[4,4,8,16,3456]{4,3,2,1,0:T(8,128)(2,1)S(1)} %slice_dynamic-update-slice_fusion) | copy-start | bytes 42467332
  139.4 11.0 %copy-start.7 = (bf16[1,4,4,128,256]{4,3,2,1,0:T(8,128)(2,1)S(1)}, bf16[1,4,4,128,256]{4,3,2,1,0:T(8,128)(2,1)}, u32[]{:S(2)}) copy-start(bf16[1,4,4,128,256]{4,3,2,1,0:T(8,128)(2,1)} %param.17) | copy-start | bytes 3145732
  146.2 21.1 %all-to-all-start.1 = ((bf16[4,4,128,256]{3,1,0,2:T(4,128)(2,1)}), bf16[4,4,128,256]{3,1,0,2:T(4,128)(2,1)S(1)}, u32[]{:S(2)}, u32[]{:S(2)}) async-start(bf16[4,4,128,256]{3,1,0,2:T(4,128)(2,1)} %copy.55), calls=%async_computation.1 | async-start | bytes 2097152 | tf_op jit(solution)/shard_map/all_to_all | solution.py:120
  150.4 18.5 %copy-start.8 = (bf16[256,256]{1,0:T(8,128)(2,1)S(1)}, bf16[256,256]{1,0:T(8,128)(2,1)}, u32[]{:S(2)}) copy-start(bf16[256,256]{1,0:T(8,128)(2,1)} %param.16) | copy-start | bytes 393220
  150.4 18.5 %copy-start.9 = (f32[4]{0:T(128)S(1)}, f32[4]{0:T(128)}, u32[]{:S(2)}) copy-start(f32[4]{0:T(128)} %param.13) | copy-start | bytes 52
  168.9 172.1 %copy-start.5 = (u32[128]{0:T(128)S(1)}, u32[128]{0:T(128)}, u32[]{:S(2)}) copy-start(u32[128]{0:T(128)} %constant.55) | copy-start | bytes 1540
  247.2 139.1 %copy-start.1 = (bf16[3456,256]{1,0:T(8,128)(2,1)S(1)}, bf16[3456,256]{1,0:T(8,128)(2,1)}, u32[]{:S(2)}) copy-start(bf16[3456,256]{1,0:T(8,128)(2,1)} %param.14) | copy-start | bytes 5308420
  250.4 93.2 %all-to-all-start.2 = ((bf16[128,4,4,256]{3,2,1,0:T(4,128)(2,1)}), bf16[128,4,4,256]{3,2,1,0:T(4,128)(2,1)S(1)}, u32[]{:S(2)}, u32[]{:S(2)}) async-start(bf16[128,4,4,256]{3,2,1,0:T(4,128)(2,1)} %bitcast.96), calls=%async_computation.2 | async-start | bytes 2097152 | tf_op jit(solution)/shard_map/all_to_all | solution.py:151
  254.3 130.5 %all-reduce.5.cloned.1.call-start = ((), (), s32[]{:S(2)}) async-start(), calls=%async_computation.3 | async-start | bytes 229376 | tf_op jit(solution)/shard_map/psum | solution.py:119
  338.4 4.0 %collective-permute-start = (f32[112,256]{1,0:T(8,128)S(1)}, f32[112,256]{1,0:T(8,128)S(1)}, u32[]{:S(2)}, u32[]{:S(2)}) collective-permute-start(f32[112,256]{1,0:T(8,128)S(1)} %fusion.2), channel_id=1, source_target_pairs={{0,1},{1,2},{2,3},{3,4},{4,5},{5,6},{6,7},{7,8},{8,9},{9,10},{10,1... | collective-permute-start | bytes 344072
  339.7 2.7 collective-permute-start.1
Sparse Core Ops, SparseCore 0:
  343.7 41.0 all-reduce.4
